TPU v7x, 32 devices: a whole 2x2x4 slice. The times are simulated.
32 devices in a mesh: row: 8 (over y, x, core), col: 4 (over z).
Axes of the slice: x: 2, y: 2, z: 4, core: 2. Of those that a mesh axis runs over, the one named last changes fastest.
Arguments:
- sub_basis: bfloat16 [32, 768, 768], P(('row', 'col')), may hold values from -0.15625 to 0.15625
- coupling: bfloat16 [32, 2, 768, 768], P(('row', 'col')), may hold values from -0.15625 to 0.15625
- pair_live: int32 [32, 2], P(('row', 'col')), may hold values 0 or 1
- offsets: int32 [32], P(('row', 'col')), may hold values from 0 to 3328
- dual_in: float32 [4, 4096], P('col', 'row'), may hold values from -6 to 6
Outputs:
- dual_out: float32 [4, 4096], P('col', 'row')
Inputs may be any that keep to these rules, and one draw needn't show every extreme that they name: `offsets`: each subdomain's window of 768 multipliers lies inside its block column's vector.
All inputs are finite; a program needn't handle non-finite values. No bound on the sum of `pair_live` on one device may be relied on, other than what follows from the above.
Results may differ from a plain program's by a relative error of at most 0.0085.
Values may be sent and summed in bfloat16 or wider, within the bound.
A program may use at most 64 MiB of HBM per device.

v0:
```python
import jax
import jax.numpy as jnp
from jax import lax
from jax.sharding import PartitionSpec as P


def passed_along(array, axis, by):
    count = lax.axis_size(axis)
    return lax.ppermute(array, axis, [(i, (i + by) % count) for i in range(count)])


def left_apply(matrix, vector):
    return lax.dot_general(
        matrix,
        vector,
        (((1,), (0,)), ((), ())),
        precision=lax.Precision.HIGHEST,
        preferred_element_type=jnp.float32,
    )


def right_apply(vector, matrix):
    return jnp.dot(
        vector, matrix, precision=lax.Precision.HIGHEST, preferred_element_type=jnp.float32
    )


def apply_dual(window, basis, couplings, live):
    projected = left_apply(basis, window)
    inner = projected
    summed = jnp.zeros_like(window)
    for slot, coupling in enumerate(couplings):
        distance = slot + 1
        ahead = passed_along(window, "col", -distance)
        inner = inner + live[slot] * left_apply(coupling, ahead)
        back = live[slot] * right_apply(projected, coupling)
        summed = summed + passed_along(back, "col", distance)
    return summed + right_apply(inner, basis)


def on_device(sub_basis, coupling, pair_live, offsets, dual_in):
    width = sub_basis.shape[2]
    basis = sub_basis[0].astype(jnp.float32)
    couplings = [coupling[0, h].astype(jnp.float32) for h in range(coupling.shape[1])]
    live = pair_live[0].astype(jnp.float32)
    length = dual_in.shape[1] * lax.axis_size("row")
    start = offsets[0]
    piece = dual_in
    for _ in range(2):
        column = lax.all_gather(piece, "row", axis=1, tiled=True)[0]
        window = lax.dynamic_slice_in_dim(column, start, width)
        local = apply_dual(window, basis, couplings, live)
        placed = lax.dynamic_update_slice(jnp.zeros((length,), jnp.float32), local, (start,))
        piece = lax.psum_scatter(placed[None, :], "row", scatter_dimension=1, tiled=True)
    return piece


def solution(mesh):
    return jax.shard_map(
        on_device,
        mesh=mesh,
        in_specs=(
            P(("row", "col"), None, None),
            P(("row", "col"), None, None, None),
            P(("row", "col"), None),
            P(("row", "col")),
            P("col", "row"),
        ),
        out_specs=P("col", "row"),
        check_vma=False,
    )
```

profile of v0, /device:TPU:0, one launch (start us, length us, event | category | flops | bytes accessed | tf_op | source)
XLA Modules:
  0.0 154.4 jit_solution(13610832899957684372)
XLA Ops:
  7.3 10.5 %all_gather.6 = f32[1,4096]{1,0:T(1,128)S(1)} all-gather(f32[1,512]{1,0:T(1,128)} %param.9), channel_id=1, replica_groups=mesh['row'=8,'col'=4] {'row'}, dimensions={1}, use_global_device_ids=true | all-gather | bytes 18432 | tf_op jit(solution)/shard_map/all_gather | solution.py:50
  17.9 3.7 %collective-permute-start.2 = (f32[768]{0:T(1024)S(1)}, f32[768]{0:T(1024)S(1)}, u32[]{:S(2)}, u32[]{:S(2)}) collective-permute-start(f32[768]{0:T(1024)S(1)} %dynamic-slice_reduce_fusion.1), channel_id=1, source_target_pairs={{0,3},{1,0},{2,1},{3,2},{4,7},{5,4},{6,5},{7,6},{8,11},{9,8},{10,9... | collective-permute-start | bytes 9224 | tf_op jit(solution)/shard_map/ppermute | solution.py:9
  21.5 1.1 fusion.73
  23.2 1.9 %fusion.30 = f32[768]{0:T(1024)S(1)} fusion(bf16[1,2,768,768]{3,2,1,0:T(8,128)(2,1)} %param.6, f32[1,768]{1,0:T(1,128)S(1)} %get-tuple-element.8), kind=kOutput, calls=%fused_computation.26 | convolution fusion | flops 7077888 | bytes 1185792 | tf_op jit(solution)/shard_map/dot_general | solution.py:23
  25.8 1.1 collective-permute-start
  28.0 2.0 %collective-permute-start.1 = (f32[768]{0:T(1024)S(1)}, f32[768]{0:T(1024)S(1)}, u32[]{:S(2)}, u32[]{:S(2)}) collective-permute-start(f32[768]{0:T(1024)S(1)} %broadcast_multiply_fusion.1), channel_id=1, source_target_pairs={{0,2},{1,3},{2,0},{3,1},{4,6},{5,7},{6,4},{7,5},{8,10},{9,11},{10,... | collective-permute-start | bytes 9224 | tf_op jit(solution)/shard_map/ppermute | solution.py:9
  30.0 1.1 fusion.33
  31.1 1.1 fusion.45
  32.2 1.2 multiply_add_fusion.1
  34.6 0.8 dynamic_update_slice.8
  35.5 2.0 %copy.6 = f32[1,4096]{0,1:T(8,128)} copy(f32[1,4096]{1,0:T(1,128)S(1)} %dynamic_update_slice.8) | data formatting | bytes 32768
  37.5 41.0 %reduce-scatter.7.cloned.1.call-done = f32[512,1]{1,0:T(8,128)} async-done(((f32[4096,1]{1,0:T(8,128)}), f32[512,1]{1,0:T(8,128)}) %reduce-scatter.7.cloned.1.call-update) | async-done | bytes 2064
  78.6 1.1 copy.7
  79.6 8.8 %all_gather.7 = f32[1,4096]{1,0:T(1,128)S(1)} all-gather(f32[1,512]{1,0:T(1,128)S(1)} %copy.7), channel_id=1, replica_groups=mesh['row'=8,'col'=4] {'row'}, dimensions={1}, use_global_device_ids=true | all-gather | bytes 18432 | tf_op jit(solution)/shard_map/all_gather | solution.py:50
  88.6 3.4 %collective-permute-start.6 = (f32[768]{0:T(1024)S(1)}, f32[768]{0:T(1024)S(1)}, u32[]{:S(2)}, u32[]{:S(2)}) collective-permute-start(f32[768]{0:T(1024)S(1)} %dynamic-slice_reduce_fusion), channel_id=1, source_target_pairs={{0,3},{1,0},{2,1},{3,2},{4,7},{5,4},{6,5},{7,6},{8,11},{9,8},{10,9... | collective-permute-start | bytes 9224 | tf_op jit(solution)/shard_map/ppermute | solution.py:9
  91.9 1.1 fusion.74
  94.9 1.1 collective-permute-start.4
  96.6 1.9 %collective-permute-start.5 = (f32[768]{0:T(1024)S(1)}, f32[768]{0:T(1024)S(1)}, u32[]{:S(2)}, u32[]{:S(2)}) collective-permute-start(f32[768]{0:T(1024)S(1)} %broadcast_multiply_fusion), channel_id=1, source_target_pairs={{0,2},{1,3},{2,0},{3,1},{4,6},{5,7},{6,4},{7,5},{8,10},{9,11},{10,... | collective-permute-start | bytes 9224 | tf_op jit(solution)/shard_map/ppermute | solution.py:9
  98.5 1.1 fusion.39
  99.6 1.1 fusion.51
  100.7 1.2 multiply_add_fusion
  102.8 2.0 %copy.8 = f32[1,4096]{0,1:T(8,128)} copy(f32[1,4096]{1,0:T(1,128)S(1)} %dynamic_update_slice.9) | data formatting | bytes 32768
  104.8 41.1 %reduce-scatter.9.cloned.1.call-done = f32[512,1]{1,0:T(8,128)} async-done(((f32[4096,1]{1,0:T(8,128)}), f32[512,1]{1,0:T(8,128)}) %reduce-scatter.9.cloned.1.call-update) | async-done | bytes 2064
  145.9 1.6 %copy.9 = f32[1,512]{1,0:T(1,128)} copy(f32[1,512]{0,1:T(8,128)} %bitcast.90) | data formatting | bytes 4096
  (46 shorter events, 7.1 us)
Async XLA Ops:
  6.5 15.0 %copy-start = (bf16[1,768,768]{2,1,0:T(8,128)(2,1)S(1)}, bf16[1,768,768]{2,1,0:T(8,128)(2,1)}, u32[]{:S(2)}) copy-start(bf16[1,768,768]{2,1,0:T(8,128)(2,1)} %param.5) | copy-start | bytes 3538948
  6.5 72.0 %reduce-scatter.7.cloned.1.call-start = ((), (), s32[]{:S(2)}) async-start(), calls=%async_computation.2 | async-start | bytes 2359296
  17.8 4.9 %copy-start.2 = (s32[1,2]{1,0:T(1,128)S(1)}, s32[1,2]{1,0:T(1,128)}, u32[]{:S(2)}) copy-start(s32[1,2]{1,0:T(1,128)} %param.7) | copy-start | bytes 28
  17.9 9.0 %copy-start.1 = (bf16[1,2,768,768]{3,2,1,0:T(8,128)(2,1)S(1)}, bf16[1,2,768,768]{3,2,1,0:T(8,128)(2,1)}, u32[]{:S(2)}) copy-start(bf16[1,2,768,768]{3,2,1,0:T(8,128)(2,1)} %param.6) | copy-start | bytes 7077892
  17.9 12.1 %collective-permute-start.2 = (f32[768]{0:T(1024)S(1)}, f32[768]{0:T(1024)S(1)}, u32[]{:S(2)}, u32[]{:S(2)}) collective-permute-start(f32[768]{0:T(1024)S(1)} %dynamic-slice_reduce_fusion.1), channel_id=1, source_target_pairs={{0,3},{1,0},{2,1},{3,2},{4,7},{5,4},{6,5},{7,6},{8,11},{9,8},{10,9... | collective-permute-start | bytes 9224 | tf_op jit(solution)/shard_map/ppermute | solution.py:9
  21.5 9.5 %collective-permute-start.3 = (f32[768]{0:T(1024)S(1)}, f32[768]{0:T(1024)S(1)}, u32[]{:S(2)}, u32[]{:S(2)}) collective-permute-start(f32[768]{0:T(1024)S(1)} %dynamic-slice_reduce_fusion.1), channel_id=1, source_target_pairs={{0,2},{1,3},{2,0},{3,1},{4,6},{5,7},{6,4},{7,5},{8,10},{9,11},{10,... | collective-permute-start | bytes 9224 | tf_op jit(solution)/shard_map/ppermute | solution.py:9
  25.8 8.2 %collective-permute-start = (f32[768]{0:T(1024)S(1)}, f32[768]{0:T(1024)S(1)}, u32[]{:S(2)}, u32[]{:S(2)}) collective-permute-start(f32[768]{0:T(1024)S(1)} %broadcast_multiply_fusion.3), channel_id=1, source_target_pairs={{0,1},{1,2},{2,3},{3,0},{4,5},{5,6},{6,7},{7,4},{8,9},{9,10},{10,1... | collective-permute-start | bytes 9224 | tf_op jit(solution)/shard_map/ppermute | solution.py:9
  28.0 6.0 %collective-permute-start.1 = (f32[768]{0:T(1024)S(1)}, f32[768]{0:T(1024)S(1)}, u32[]{:S(2)}, u32[]{:S(2)}) collective-permute-start(f32[768]{0:T(1024)S(1)} %broadcast_multiply_fusion.1), channel_id=1, source_target_pairs={{0,2},{1,3},{2,0},{3,1},{4,6},{5,7},{6,4},{7,5},{8,10},{9,11},{10,... | collective-permute-start | bytes 9224 | tf_op jit(solution)/shard_map/ppermute | solution.py:9
  37.5 108.4 %reduce-scatter.9.cloned.1.call-start = ((), (), s32[]{:S(2)}) async-start(), calls=%async_computation.3 | async-start | bytes 2359296
  88.6 10.0 %collective-permute-start.6 = (f32[768]{0:T(1024)S(1)}, f32[768]{0:T(1024)S(1)}, u32[]{:S(2)}, u32[]{:S(2)}) collective-permute-start(f32[768]{0:T(1024)S(1)} %dynamic-slice_reduce_fusion), channel_id=1, source_target_pairs={{0,3},{1,0},{2,1},{3,2},{4,7},{5,4},{6,5},{7,6},{8,11},{9,8},{10,9... | collective-permute-start | bytes 9224 | tf_op jit(solution)/shard_map/ppermute | solution.py:9
  91.9 7.7 %collective-permute-start.7 = (f32[768]{0:T(1024)S(1)}, f32[768]{0:T(1024)S(1)}, u32[]{:S(2)}, u32[]{:S(2)}) collective-permute-start(f32[768]{0:T(1024)S(1)} %dynamic-slice_reduce_fusion), channel_id=1, source_target_pairs={{0,2},{1,3},{2,0},{3,1},{4,6},{5,7},{6,4},{7,5},{8,10},{9,11},{10,... | collective-permute-start | bytes 9224 | tf_op jit(solution)/shard_map/ppermute | solution.py:9
  94.9 7.6 %collective-permute-start.4 = (f32[768]{0:T(1024)S(1)}, f32[768]{0:T(1024)S(1)}, u32[]{:S(2)}, u32[]{:S(2)}) collective-permute-start(f32[768]{0:T(1024)S(1)} %broadcast_multiply_fusion.2), channel_id=1, source_target_pairs={{0,1},{1,2},{2,3},{3,0},{4,5},{5,6},{6,7},{7,4},{8,9},{9,10},{10,1... | collective-permute-start | bytes 9224 | tf_op jit(solution)/shard_map/ppermute | solution.py:9
  96.6 5.9 %collective-permute-start.5 = (f32[768]{0:T(1024)S(1)}, f32[768]{0:T(1024)S(1)}, u32[]{:S(2)}, u32[]{:S(2)}) collective-permute-start(f32[768]{0:T(1024)S(1)} %broadcast_multiply_fusion), channel_id=1, source_target_pairs={{0,2},{1,3},{2,0},{3,1},{4,6},{5,7},{6,4},{7,5},{8,10},{9,11},{10,... | collective-permute-start | bytes 9224 | tf_op jit(solution)/shard_map/ppermute | solution.py:9
Sparse Core Ops, SparseCore 0:
  37.6 40.9 reduce-scatter.6
  104.9 40.9 reduce-scatter.8
where the time goes:
time: 155 us; the launch traced here: 154 us
  waiting for transfers between devices  82.2 us (53%)
  blocking collectives  19.3 us (12%)
  between operations  14.5 us (9%)
  starting transfers between devices  13.2 us (9%)
  matrix products  11.3 us (7%)
  local copies, waits for them, and re-layouts  9.11 us (6%)
  other arithmetic  4.85 us (3%)
    unnamed x4, waiting for transfers between devices  82.2 us
    all_gather x2, blocking collectives, on_device(): column = lax.all_gather(piece, 'row', axis=1, tiled=True)[0]  19.3 us
    ppermute x8, starting transfers between devices, passed_along(): lax.ppermute(array, axis, [(i, (i + by) % count) for i in range(count)])  13.1 us
    unnamed x10, local copies, waits for them, and re-layouts  6.72 us
    dot_general x6, matrix products, left_apply(): lax.dot_general(matrix, vector, (((1,), (0,)), ((), ())), precision=lax.P...  6.42 us
    dot_general x6, matrix products, right_apply(): jnp.dot(vector, matrix, precision=lax.Precision.HIGHEST, preferred_elemen...  4.84 us
  transfers between devices with their start and end apart: 10, of which 2 were waited for; matrix products, arithmetic and copies ran while one was open for 11% of the time, Pallas kernels for 0%

commit v1 on v0

--- a/solution.py
+++ b/solution.py
@@ -2,6 +2,18 @@
 import jax.numpy as jnp
 from jax import lax
 from jax.sharding import PartitionSpec as P
+
+
+def gather_by_bits(array, axis, dim):
+    ways, here = (lax.axis_size(axis), lax.axis_index(axis))
+    grown, reach = (array, 1)
+    while reach < ways:
+        theirs = lax.ppermute(grown, axis, [(d, d ^ reach) for d in range(ways)])
+        mine_first = jnp.concatenate([grown, theirs], axis=dim)
+        theirs_first = jnp.concatenate([theirs, grown], axis=dim)
+        grown = jnp.where(here & reach == 0, mine_first, theirs_first)
+        reach = 2 * reach
+    return grown
 
 
 def passed_along(array, axis, by):
@@ -47,7 +59,7 @@
     start = offsets[0]
     piece = dual_in
     for _ in range(2):
-        column = lax.all_gather(piece, "row", axis=1, tiled=True)[0]
+        column = gather_by_bits(piece, "row", 1)[0]
         window = lax.dynamic_slice_in_dim(column, start, width)
         local = apply_dual(window, basis, couplings, live)
         placed = lax.dynamic_update_slice(jnp.zeros((length,), jnp.float32), local, (start,))

time: 155 us -> 155 us (level)
  blocking collectives: 19.3 us -> 0 us
  waiting for transfers between devices: 82.2 us -> 91.2 us
  starting transfers between devices: 13.2 us -> 21.8 us
  other arithmetic: 4.85 us -> 7.2 us
    all_gather x2 -> x0, blocking collectives: 19.3 us -> none  [on_device(): column = lax.all_gather(piece, 'row', axis=1, tiled=True)[0]]
    ppermute x0 -> x6, starting transfers between devices: none -> 8.13 us  [gather_by_bits(): theirs = lax.ppermute(grown, axis, [(d, d ^ reach) for d in range(ways)])]
    ppermute x0 -> x6, waiting for transfers between devices: none -> 7.97 us  [gather_by_bits(): theirs = lax.ppermute(grown, axis, [(d, d ^ reach) for d in range(ways)])]
    select_n x0 -> x8, other arithmetic: none -> 1.57 us  [gather_by_bits(): grown = jnp.where(here & reach == 0, mine_first, theirs_first)]
    unnamed x10 -> x8, local copies, waits for them, and re-layouts: 6.72 us -> 6.71 us
  transfers between devices with their start and end apart: 10 -> 16, of which waited for: 2 -> 7; matrix products, arithmetic and copies ran while one was open for 11% -> 12% of each run, Pallas kernels for 0% -> 0%
where the time goes in v1:
time: 155 us
  waiting for transfers between devices  91.2 us (59%)
  starting transfers between devices  21.8 us (14%)
  between operations  14.4 us (9%)
  matrix products  11.2 us (7%)
  local copies, waits for them, and re-layouts  8.94 us (6%)
  other arithmetic  7.2 us (5%)
    unnamed x4, waiting for transfers between devices  83.2 us
    ppermute x8, starting transfers between devices, passed_along(): lax.ppermute(array, axis, [(i, (i + by) % count) for i in range(count)])  13.6 us
    ppermute x6, starting transfers between devices, gather_by_bits(): theirs = lax.ppermute(grown, axis, [(d, d ^ reach) for d in range(ways)])  8.13 us
    ppermute x6, waiting for transfers between devices, gather_by_bits(): theirs = lax.ppermute(grown, axis, [(d, d ^ reach) for d in range(ways)])  7.97 us
    unnamed x8, local copies, waits for them, and re-layouts  6.71 us
    dot_general x6, matrix products, left_apply(): lax.dot_general(matrix, vector, (((1,), (0,)), ((), ())), precision=lax.P...  6.39 us
    dot_general x6, matrix products, right_apply(): jnp.dot(vector, matrix, precision=lax.Precision.HIGHEST, preferred_elemen...  4.85 us
  transfers between devices with their start and end apart: 16, of which 7 were waited for; matrix products, arithmetic and copies ran while one was open for 12% of the time, Pallas kernels for 0%

profile of v1, /device:TPU:0, one launch (start us, length us, event | category | flops | bytes accessed | tf_op | source)
XLA Modules:
  0.0 154.7 jit_solution(4331321858795208120)
XLA Ops:
  9.7 2.6 %collective-permute-start.1 = (f32[1,1024]{1,0:T(1,128)S(1)}, f32[1,1024]{1,0:T(1,128)S(1)}, u32[]{:S(2)}, u32[]{:S(2)}) collective-permute-start(f32[1,1024]{1,0:T(1,128)S(1)} %broadcast_select_fusion.3), channel_id=1, source_target_pairs={{0,8},{4,12},{8,0},{12,4},{16,24},{20,28},{24,16},{28,20},{1,9},{5... | collective-permute-start | bytes 12296 | tf_op jit(solution)/shard_map/ppermute | solution.py:11
  13.9 2.1 %collective-permute-start.2 = (f32[1,2048]{1,0:T(1,128)S(1)}, f32[1,2048]{1,0:T(1,128)S(1)}, u32[]{:S(2)}, u32[]{:S(2)}) collective-permute-start(f32[1,2048]{1,0:T(1,128)S(1)} %broadcast_select_fusion.1), channel_id=1, source_target_pairs={{0,16},{4,20},{8,24},{12,28},{16,0},{20,4},{24,8},{28,12},{1,17},{... | collective-permute-start | bytes 24584 | tf_op jit(solution)/shard_map/ppermute | solution.py:11
  16.0 1.6 %collective-permute-done.2 = f32[1,2048]{1,0:T(1,128)S(1)} collective-permute-done((f32[1,2048]{1,0:T(1,128)S(1)}, f32[1,2048]{1,0:T(1,128)S(1)}, u32[]{:S(2)}, u32[]{:S(2)}) %collective-permute-start.2) | collective-permute-done | bytes 8224 | tf_op jit(solution)/shard_map/ppermute | solution.py:11
  17.7 4.2 %collective-permute-start.5 = (f32[768]{0:T(1024)S(1)}, f32[768]{0:T(1024)S(1)}, u32[]{:S(2)}, u32[]{:S(2)}) collective-permute-start(f32[768]{0:T(1024)S(1)} %get-tuple-element.7), channel_id=1, source_target_pairs={{0,3},{1,0},{2,1},{3,2},{4,7},{5,4},{6,5},{7,6},{8,11},{9,8},{10,9... | collective-permute-start | bytes 9224 | tf_op jit(solution)/shard_map/ppermute | solution.py:21
  23.0 1.9 %fusion.30 = f32[768]{0:T(1024)S(1)} fusion(bf16[1,2,768,768]{3,2,1,0:T(8,128)(2,1)} %param.6, f32[1,768]{1,0:T(1,128)S(1)} %get-tuple-element.12), kind=kOutput, calls=%fused_computation.26 | convolution fusion | flops 7077888 | bytes 1185792 | tf_op jit(solution)/shard_map/dot_general | solution.py:35
  27.7 2.0 %collective-permute-start.4 = (f32[768]{0:T(1024)S(1)}, f32[768]{0:T(1024)S(1)}, u32[]{:S(2)}, u32[]{:S(2)}) collective-permute-start(f32[768]{0:T(1024)S(1)} %broadcast_multiply_fusion.1), channel_id=1, source_target_pairs={{0,2},{1,3},{2,0},{3,1},{4,6},{5,7},{6,4},{7,5},{8,10},{9,11},{10,... | collective-permute-start | bytes 9224 | tf_op jit(solution)/shard_map/ppermute | solution.py:21
  29.7 1.1 fusion.33
  30.8 1.1 fusion.45
  31.9 1.2 multiply_add_fusion.1
  35.2 2.0 %copy.6 = f32[1,4096]{0,1:T(8,128)} copy(f32[1,4096]{1,0:T(1,128)S(1)} %dynamic_update_slice.8) | data formatting | bytes 32768
  37.2 42.0 %reduce-scatter.7.cloned.1.call-done = f32[512,1]{1,0:T(8,128)} async-done(((f32[4096,1]{1,0:T(8,128)}), f32[512,1]{1,0:T(8,128)}) %reduce-scatter.7.cloned.1.call-update) | async-done | bytes 2064
  80.4 1.1 collective-permute-done.7
  81.5 1.4 collective-permute-start.8
  82.9 2.2 %collective-permute-done.8 = f32[1,1024]{1,0:T(1,128)S(1)} collective-permute-done((f32[1,1024]{1,0:T(1,128)S(1)}, f32[1,1024]{1,0:T(1,128)S(1)}, u32[]{:S(2)}, u32[]{:S(2)}) %collective-permute-start.8) | collective-permute-done | bytes 4128 | tf_op jit(solution)/shard_map/ppermute | solution.py:11
  85.1 1.5 collective-permute-start.9
  86.6 2.2 %collective-permute-done.9 = f32[1,2048]{1,0:T(1,128)S(1)} collective-permute-done((f32[1,2048]{1,0:T(1,128)S(1)}, f32[1,2048]{1,0:T(1,128)S(1)}, u32[]{:S(2)}, u32[]{:S(2)}) %collective-permute-start.9) | collective-permute-done | bytes 8224 | tf_op jit(solution)/shard_map/ppermute | solution.py:11
  89.0 3.4 %collective-permute-start.12 = (f32[768]{0:T(1024)S(1)}, f32[768]{0:T(1024)S(1)}, u32[]{:S(2)}, u32[]{:S(2)}) collective-permute-start(f32[768]{0:T(1024)S(1)} %get-tuple-element.5), channel_id=1, source_target_pairs={{0,3},{1,0},{2,1},{3,2},{4,7},{5,4},{6,5},{7,6},{8,11},{9,8},{10,9... | collective-permute-start | bytes 9224 | tf_op jit(solution)/shard_map/ppermute | solution.py:21
  95.2 1.1 collective-permute-start.10
  97.0 1.9 %collective-permute-start.11 = (f32[768]{0:T(1024)S(1)}, f32[768]{0:T(1024)S(1)}, u32[]{:S(2)}, u32[]{:S(2)}) collective-permute-start(f32[768]{0:T(1024)S(1)} %broadcast_multiply_fusion), channel_id=1, source_target_pairs={{0,2},{1,3},{2,0},{3,1},{4,6},{5,7},{6,4},{7,5},{8,10},{9,11},{10,... | collective-permute-start | bytes 9224 | tf_op jit(solution)/shard_map/ppermute | solution.py:21
  100.0 1.1 fusion.51
  101.1 1.2 multiply_add_fusion
  103.1 2.0 %copy.8 = f32[1,4096]{0,1:T(8,128)} copy(f32[1,4096]{1,0:T(1,128)S(1)} %dynamic_update_slice.9) | data formatting | bytes 32768
  105.1 41.1 %reduce-scatter.9.cloned.1.call-done = f32[512,1]{1,0:T(8,128)} async-done(((f32[4096,1]{1,0:T(8,128)}), f32[512,1]{1,0:T(8,128)}) %reduce-scatter.9.cloned.1.call-update) | async-done | bytes 2064
  146.3 1.6 %copy.9 = f32[1,512]{1,0:T(1,128)} copy(f32[1,512]{0,1:T(8,128)} %bitcast.100) | data formatting | bytes 4096
  (62 shorter events, 16.8 us)
Async XLA Ops:
  6.5 15.4 %copy-start = (bf16[1,768,768]{2,1,0:T(8,128)(2,1)S(1)}, bf16[1,768,768]{2,1,0:T(8,128)(2,1)}, u32[]{:S(2)}) copy-start(bf16[1,768,768]{2,1,0:T(8,128)(2,1)} %param.5) | copy-start | bytes 3538948
  6.5 72.7 %reduce-scatter.7.cloned.1.call-start = ((), (), s32[]{:S(2)}) async-start(), calls=%async_computation.2 | async-start | bytes 2359296
  6.5 2.4 %collective-permute-start = (f32[1,512]{1,0:T(1,128)}, f32[1,512]{1,0:T(1,128)S(1)}, u32[]{:S(2)}, u32[]{:S(2)}) collective-permute-start(f32[1,512]{1,0:T(1,128)} %param.9), channel_id=1, source_target_pairs={{0,4},{4,0},{8,12},{12,8},{16,20},{20,16},{24,28},{28,24},{1,5},{5... | collective-permute-start | bytes 6152 | tf_op jit(solution)/shard_map/ppermute | solution.py:11
  9.7 4.2 %collective-permute-start.1 = (f32[1,1024]{1,0:T(1,128)S(1)}, f32[1,1024]{1,0:T(1,128)S(1)}, u32[]{:S(2)}, u32[]{:S(2)}) collective-permute-start(f32[1,1024]{1,0:T(1,128)S(1)} %broadcast_select_fusion.3), channel_id=1, source_target_pairs={{0,8},{4,12},{8,0},{12,4},{16,24},{20,28},{24,16},{28,20},{1,9},{5... | collective-permute-start | bytes 12296 | tf_op jit(solution)/shard_map/ppermute | solution.py:11
  13.9 3.7 %collective-permute-start.2 = (f32[1,2048]{1,0:T(1,128)S(1)}, f32[1,2048]{1,0:T(1,128)S(1)}, u32[]{:S(2)}, u32[]{:S(2)}) collective-permute-start(f32[1,2048]{1,0:T(1,128)S(1)} %broadcast_select_fusion.1), channel_id=1, source_target_pairs={{0,16},{4,20},{8,24},{12,28},{16,0},{20,4},{24,8},{28,12},{1,17},{... | collective-permute-start | bytes 24584 | tf_op jit(solution)/shard_map/ppermute | solution.py:11
  17.7 12.0 %collective-permute-start.5 = (f32[768]{0:T(1024)S(1)}, f32[768]{0:T(1024)S(1)}, u32[]{:S(2)}, u32[]{:S(2)}) collective-permute-start(f32[768]{0:T(1024)S(1)} %get-tuple-element.7), channel_id=1, source_target_pairs={{0,3},{1,0},{2,1},{3,2},{4,7},{5,4},{6,5},{7,6},{8,11},{9,8},{10,9... | collective-permute-start | bytes 9224 | tf_op jit(solution)/shard_map/ppermute | solution.py:21
  21.9 8.9 %collective-permute-start.6 = (f32[768]{0:T(1024)S(1)}, f32[768]{0:T(1024)S(1)}, u32[]{:S(2)}, u32[]{:S(2)}) collective-permute-start(f32[768]{0:T(1024)S(1)} %get-tuple-element.7), channel_id=1, source_target_pairs={{0,2},{1,3},{2,0},{3,1},{4,6},{5,7},{6,4},{7,5},{8,10},{9,11},{10,... | collective-permute-start | bytes 9224 | tf_op jit(solution)/shard_map/ppermute | solution.py:21
  21.9 3.0 %copy-start.1 = (bf16[1,2,768,768]{3,2,1,0:T(8,128)(2,1)S(1)}, bf16[1,2,768,768]{3,2,1,0:T(8,128)(2,1)}, u32[]{:S(2)}) copy-start(bf16[1,2,768,768]{3,2,1,0:T(8,128)(2,1)} %param.6) | copy-start | bytes 7077892
  26.0 7.7 %collective-permute-start.3 = (f32[768]{0:T(1024)S(1)}, f32[768]{0:T(1024)S(1)}, u32[]{:S(2)}, u32[]{:S(2)}) collective-permute-start(f32[768]{0:T(1024)S(1)} %broadcast_multiply_fusion.3), channel_id=1, source_target_pairs={{0,1},{1,2},{2,3},{3,0},{4,5},{5,6},{6,7},{7,4},{8,9},{9,10},{10,1... | collective-permute-start | bytes 9224 | tf_op jit(solution)/shard_map/ppermute | solution.py:21
  27.7 6.0 %collective-permute-start.4 = (f32[768]{0:T(1024)S(1)}, f32[768]{0:T(1024)S(1)}, u32[]{:S(2)}, u32[]{:S(2)}) collective-permute-start(f32[768]{0:T(1024)S(1)} %broadcast_multiply_fusion.1), channel_id=1, source_target_pairs={{0,2},{1,3},{2,0},{3,1},{4,6},{5,7},{6,4},{7,5},{8,10},{9,11},{10,... | collective-permute-start | bytes 9224 | tf_op jit(solution)/shard_map/ppermute | solution.py:21
  37.2 109.1 %reduce-scatter.9.cloned.1.call-start = ((), (), s32[]{:S(2)}) async-start(), calls=%async_computation.3 | async-start | bytes 2359296
  80.3 1.2 collective-permute-start.7
  81.5 3.6 %collective-permute-start.8 = (f32[1,1024]{1,0:T(1,128)S(1)}, f32[1,1024]{1,0:T(1,128)S(1)}, u32[]{:S(2)}, u32[]{:S(2)}) collective-permute-start(f32[1,1024]{1,0:T(1,128)S(1)} %broadcast_select_fusion.2), channel_id=1, source_target_pairs={{0,8},{4,12},{8,0},{12,4},{16,24},{20,28},{24,16},{28,20},{1,9},{5... | collective-permute-start | bytes 12296 | tf_op jit(solution)/shard_map/ppermute | solution.py:11
  85.1 3.7 %collective-permute-start.9 = (f32[1,2048]{1,0:T(1,128)S(1)}, f32[1,2048]{1,0:T(1,128)S(1)}, u32[]{:S(2)}, u32[]{:S(2)}) collective-permute-start(f32[1,2048]{1,0:T(1,128)S(1)} %broadcast_select_fusion), channel_id=1, source_target_pairs={{0,16},{4,20},{8,24},{12,28},{16,0},{20,4},{24,8},{28,12},{1,17},{... | collective-permute-start | bytes 24584 | tf_op jit(solution)/shard_map/ppermute | solution.py:11
  89.0 9.9 %collective-permute-start.12 = (f32[768]{0:T(1024)S(1)}, f32[768]{0:T(1024)S(1)}, u32[]{:S(2)}, u32[]{:S(2)}) collective-permute-start(f32[768]{0:T(1024)S(1)} %get-tuple-element.5), channel_id=1, source_target_pairs={{0,3},{1,0},{2,1},{3,2},{4,7},{5,4},{6,5},{7,6},{8,11},{9,8},{10,9... | collective-permute-start | bytes 9224 | tf_op jit(solution)/shard_map/ppermute | solution.py:21
  92.3 7.6 %collective-permute-start.13 = (f32[768]{0:T(1024)S(1)}, f32[768]{0:T(1024)S(1)}, u32[]{:S(2)}, u32[]{:S(2)}) collective-permute-start(f32[768]{0:T(1024)S(1)} %get-tuple-element.5), channel_id=1, source_target_pairs={{0,2},{1,3},{2,0},{3,1},{4,6},{5,7},{6,4},{7,5},{8,10},{9,11},{10,... | collective-permute-start | bytes 9224 | tf_op jit(solution)/shard_map/ppermute | solution.py:21
  95.2 7.7 %collective-permute-start.10 = (f32[768]{0:T(1024)S(1)}, f32[768]{0:T(1024)S(1)}, u32[]{:S(2)}, u32[]{:S(2)}) collective-permute-start(f32[768]{0:T(1024)S(1)} %broadcast_multiply_fusion.2), channel_id=1, source_target_pairs={{0,1},{1,2},{2,3},{3,0},{4,5},{5,6},{6,7},{7,4},{8,9},{9,10},{10,1... | collective-permute-start | bytes 9224 | tf_op jit(solution)/shard_map/ppermute | solution.py:21
  97.0 5.9 %collective-permute-start.11 = (f32[768]{0:T(1024)S(1)}, f32[768]{0:T(1024)S(1)}, u32[]{:S(2)}, u32[]{:S(2)}) collective-permute-start(f32[768]{0:T(1024)S(1)} %broadcast_multiply_fusion), channel_id=1, source_target_pairs={{0,2},{1,3},{2,0},{3,1},{4,6},{5,7},{6,4},{7,5},{8,10},{9,11},{10,... | collective-permute-start | bytes 9224 | tf_op jit(solution)/shard_map/ppermute | solution.py:21
Sparse Core Ops, SparseCore 0:
  37.3 41.8 reduce-scatter.6
  105.3 40.9 reduce-scatter.8
